TPU v7x, 256 devices: a whole 4x4x8 slice. The times are simulated.
256 devices in a mesh: seq: 32 (over x, z), head: 8 (over y, core).
Axes of the slice: x: 4, y: 4, z: 8, core: 2. Of those that a mesh axis runs over, the one named last changes fastest.
Arguments:
- queries: bfloat16 [8192, 4096], P('seq', 'head'), may hold values from -8 to 8
- suffix_key_value: bfloat16 [8192, 2, 2048], P('seq', None, 'head'), may hold values from -8 to 8
- pooled_pages: bfloat16 [512, 256, 2, 2048], P('seq', None, None, 'head'), may hold values from -8 to 8
- out_weight: bfloat16 [4096, 5376], P('head'), may hold values from -0.5 to 0.5
- page_table: int32 [16, 32], replicated, may hold values from 0 to 511, as said below
- prefix_len: int32 [16], replicated, may hold values from 1024 to 8192, as said below
- suffix_len: int32 [16], replicated, may hold values from 2 to 512, as said below
Outputs:
- projected: bfloat16 [8192, 5376], P('seq', 'head')
Inputs may be any that keep to these rules, and one draw needn't show every extreme that they name: `page_table`: every slot of the pool appears exactly once; slot s lies on index s // 16 of seq, and every index of seq holds exactly 1 pages of every request. `prefix_len`: some request has exactly 8192 prefix tokens. `suffix_len`: some request has exactly 512 live suffix tokens.
All inputs are finite; a program needn't handle non-finite values.
Results may differ from a plain program's by a relative error of at most 0.013.
Values may be sent and summed in bfloat16 or wider, within the bound.
A program may use at most 128 MiB of HBM per device.

v0:
```python
import jax
import jax.numpy as jnp
from jax import lax
from jax.sharding import PartitionSpec as P

D = 5376
QUERY_HEADS = 32
KEY_VALUE_HEADS = 16
HEAD_WIDTH = 128


def shifted(x, axis, by):
    devices = lax.axis_size(axis)
    pairs = [(i, i + by) for i in range(devices) if 0 <= i + by < devices]
    return lax.ppermute(x, axis, pairs)


def page_ranks(page_table, pages_dev):
    owners = page_table // pages_dev
    earlier = (owners[:, :, None] == owners[:, None, :]) & (
        page_table[:, None, :] < page_table[:, :, None]
    )
    return (owners, jnp.sum(earlier.astype(jnp.int32), axis=2))


def pack_pages(pooled_pages, kept_pages, slot_of, local_slot, slot_width):
    columns = jnp.arange(slot_width, dtype=jnp.int32)
    matched = kept_pages[:, None, :] & (slot_of[:, None, :] == columns[None, :, None])
    chosen_slot = jnp.sum(jnp.where(matched, local_slot[:, None, :], 0), axis=2).reshape(-1)
    filled = jnp.any(matched, axis=2).reshape(-1)
    chosen = jnp.take(pooled_pages, chosen_slot, axis=0)
    return jnp.where(filled[:, None, None, None], chosen, jnp.zeros_like(chosen))


def page_mask(my_owners, slot_of, wanted, seq_count, slot_width, rows_of_pages, my_prefix):
    sources = jnp.arange(seq_count, dtype=jnp.int32)
    columns = jnp.arange(slot_width, dtype=jnp.int32)
    matched = (
        wanted[:, None, :]
        & (my_owners[None, None, :] == sources[:, None, None])
        & (slot_of[None, None, :] == columns[None, :, None])
    )
    page_index = jnp.arange(my_owners.shape[0], dtype=jnp.int32)
    first_row = jnp.sum(jnp.where(matched, page_index[None, None, :], 0), axis=2) * rows_of_pages
    filled = jnp.any(matched, axis=2)
    offsets = jnp.arange(rows_of_pages, dtype=jnp.int32)
    positions = first_row[:, :, None] + offsets[None, None, :]
    return (filled[:, :, None] & (positions < my_prefix)).reshape(1, -1)


def attend(query_head, key_parts, score_scale):
    tok_rows = query_head.shape[0]
    group_of_heads = query_head.shape[1]
    head_size = query_head.shape[2]
    flat_query = query_head.reshape(tok_rows * group_of_heads, head_size)
    score_list = []
    row_max = None
    for key_rows, value_rows, visible in key_parts:
        scores = jnp.einsum("qd,spd->qsp", flat_query, key_rows, preferred_element_type=jnp.float32)
        scores = scores.reshape(tok_rows, group_of_heads, -1) * score_scale
        part_max = jnp.max(jnp.where(visible[:, None, :], scores, -jnp.inf), axis=2)
        row_max = part_max if row_max is None else jnp.maximum(row_max, part_max)
        score_list.append(scores)
    row_total = jnp.zeros((tok_rows, group_of_heads), jnp.float32)
    mixed_sum = jnp.zeros((tok_rows, group_of_heads, head_size), jnp.float32)
    for (key_rows, value_rows, visible), scores in zip(key_parts, score_list):
        weights = jnp.where(visible[:, None, :], jnp.exp(scores - row_max[:, :, None]), 0.0)
        row_total = row_total + jnp.sum(weights, axis=2)
        rounded = weights.astype(jnp.bfloat16).reshape(
            tok_rows * group_of_heads, value_rows.shape[0], value_rows.shape[1]
        )
        product = jnp.einsum("qsp,spd->qd", rounded, value_rows, preferred_element_type=jnp.float32)
        mixed_sum = mixed_sum + product.reshape(tok_rows, group_of_heads, head_size)
    return mixed_sum / row_total[:, :, None]


def shards(queries, suffix_key_value, pooled_pages, out_weight, page_table, prefix_len, suffix_len):
    tok_rows = queries.shape[0]
    pages_dev = pooled_pages.shape[0]
    rows_of_pages = pooled_pages.shape[1]
    kv_local = suffix_key_value.shape[2] // HEAD_WIDTH
    group_of_heads = QUERY_HEADS // KEY_VALUE_HEADS
    score_scale = float(D // QUERY_HEADS) ** (-0.5)
    seq_count = lax.axis_size("seq")
    half_count = seq_count // 2
    seq_index = lax.axis_index("seq")
    member = seq_index // half_count
    request = seq_index % half_count
    holding = 2 * pages_dev // seq_count
    owners, rank_table = page_ranks(page_table, pages_dev)
    picked = jnp.arange(page_table.shape[0], dtype=jnp.int32) == request
    my_prefix = jnp.sum(jnp.where(picked, prefix_len, 0))
    my_suffix = jnp.sum(jnp.where(picked, suffix_len, 0))
    my_owners = jnp.sum(jnp.where(picked[:, None], owners, 0), axis=0)
    my_ranks = jnp.sum(jnp.where(picked[:, None], rank_table, 0), axis=0)
    send_owners = jnp.concatenate([owners, owners], axis=0)
    send_ranks = jnp.concatenate([rank_table, rank_table], axis=0)
    slot_table = page_table % pages_dev
    send_slots = jnp.concatenate([slot_table, slot_table], axis=0)
    held_here = send_owners == seq_index
    previous = shifted(suffix_key_value, "seq", half_count)
    suffix_rows = jnp.concatenate([previous, suffix_key_value], axis=0)
    query_pos = member * tok_rows + jnp.arange(tok_rows, dtype=jnp.int32)
    key_index = jnp.arange(2 * tok_rows, dtype=jnp.int32)
    own_pos = member * tok_rows + key_index - tok_rows
    earlier_part = (key_index < tok_rows) & (member == 1) & (key_index < my_suffix)
    later_part = (key_index >= tok_rows) & (own_pos < my_suffix)
    suffix_visible = earlier_part[None, :] | later_part[None, :] & (
        own_pos[None, :] <= query_pos[:, None]
    )
    outgoing = pack_pages(pooled_pages, held_here, send_ranks, send_slots, holding)
    received = lax.all_to_all(outgoing, "seq", split_axis=0, concat_axis=0, tiled=True)
    all_sources = jnp.ones((seq_count, my_owners.shape[0]), dtype=jnp.bool_)
    page_parts = [
        (
            received,
            page_mask(
                my_owners, my_ranks, all_sources, seq_count, holding, rows_of_pages, my_prefix
            ),
        )
    ]
    query_layout = queries.reshape(tok_rows, kv_local, group_of_heads, HEAD_WIDTH)
    heads_out = []
    for head_slot in range(kv_local):
        head_start = head_slot * HEAD_WIDTH
        head_stop = head_start + HEAD_WIDTH
        key_parts = [
            (
                page_block[:, :, 0, head_start:head_stop],
                page_block[:, :, 1, head_start:head_stop],
                visible,
            )
            for page_block, visible in page_parts
        ]
        key_parts.append(
            (
                suffix_rows[None, :, 0, head_start:head_stop],
                suffix_rows[None, :, 1, head_start:head_stop],
                suffix_visible,
            )
        )
        heads_out.append(attend(query_layout[:, head_slot], key_parts, score_scale))
    attention = jnp.stack(heads_out, axis=1)
    live_query = (query_pos < my_suffix)[:, None, None, None]
    attention = jnp.where(live_query, attention, 0.0).astype(jnp.bfloat16).reshape(tok_rows, -1)
    partial_value = jnp.dot(attention, out_weight, preferred_element_type=jnp.float32)
    summed = lax.psum_scatter(
        partial_value.astype(jnp.bfloat16), "head", scatter_dimension=1, tiled=True
    )
    return summed


def solution(mesh):
    placed = (
        P("seq", "head"),
        P("seq", None, "head"),
        P("seq", None, None, "head"),
        P("head", None),
        P(),
        P(),
        P(),
    )
    return jax.shard_map(
        shards, mesh=mesh, in_specs=placed, out_specs=P("seq", "head"), check_vma=False
    )
```

profile of v0, /device:TPU:3, one launch (start us, length us, event | category | flops | bytes accessed | tf_op | source)
XLA Modules:
  0.0 401.7 jit_solution(17475658564496521093)
XLA Ops:
  6.5 0.7 add_select_fusion.2
  7.2 1.3 convert_reduce_fusion
  8.7 20.6 %gather_fusion = bf16[32,256,2,256]{3,2,1,0:T(2,128)(2,1)} fusion(bf16[16,256,2,256]{3,2,1,0:T(2,128)(2,1)} %param.9, s32[1024]{0:T(1024)S(1)} %pad_clamp_fusion), kind=kCustom, calls=%fused_computation | custom fusion | bytes 16777344 | tf_op jit(solution)/shard_map/jit(_take)/gather | solution.py:31
  29.4 11.6 %broadcast_select_fusion.1 = bf16[32,256,2,256]{3,2,1,0:T(2,128)(2,1)} fusion(pred[32]{0:T(512)(128)(4,1)S(1)} %reduce_or.19, bf16[32,256,2,256]{3,2,1,0:T(2,128)(2,1)} %gather_fusion, pred[32]{0:T(512)(128)(4,1)S(1)} %compare_and_fusion), kind=kLoop, calls=%fused_computation.12 | loop fusion | flops 8388608 | bytes 16777280 | tf_op jit(solution)/shard_map/jit(_where)/select_n | solution.py:32
  40.9 8.3 %copy.67 = bf16[32,256,2,256]{3,1,2,0:T(8,128)(2,1)} copy(bf16[32,256,2,256]{3,2,1,0:T(2,128)(2,1)} %broadcast_select_fusion.1) | data formatting | bytes 16777216 | tf_op jit(solution)/shard_map/jit(_where)/select_n | solution.py:32
  49.3 11.3 %all-to-all-start = ((bf16[32,256,2,256]{3,1,2,0:T(8,128)(2,1)}), bf16[32,256,2,256]{3,1,2,0:T(8,128)(2,1)}, u32[]{:S(2)}, u32[]{:S(2)}) async-start(bf16[32,256,2,256]{3,1,2,0:T(8,128)(2,1)} %copy.67), calls=%async_computation | async-start | bytes 16777216 | tf_op jit(solution)/shard_map/all_to_all | solution.py:112
  60.6 3.9 collective-permute-start
  64.8 0.6 select_reduce_fusion.9
  66.9 0.7 fusion.36
  67.7 0.7 fusion.35
  68.4 0.6 fusion.45
  69.5 13.2 %collective-permute-done = bf16[256,2,256]{2,0,1:T(8,128)(2,1)S(1)} collective-permute-done((bf16[256,2,256]{2,0,1:T(8,128)(2,1)S(1)}, bf16[256,2,256]{2,0,1:T(8,128)(2,1)S(1)}, u32[]{:S(2)}, u32[]{:S(2)}) %collective-permute-start) | collective-permute-done | bytes 262176 | tf_op jit(solution)/shard_map/ppermute | solution.py:15
  83.3 160.6 %all-to-all-done = bf16[32,256,2,256]{3,1,2,0:T(8,128)(2,1)} async-done(((bf16[32,256,2,256]{3,1,2,0:T(8,128)(2,1)}), bf16[32,256,2,256]{3,1,2,0:T(8,128)(2,1)}, u32[]{:S(2)}, u32[]{:S(2)}) %all-to-all-start) | async-done | bytes 8388640 | tf_op jit(solution)/shard_map/all_to_all | solution.py:112
  244.0 7.8 %select_reduce_fusion.3 = (f32[512]{0:T(512)S(1)}, f32[32,256,512]{2,1,0:T(8,128)}) fusion(pred[32,256]{1,0:T(8,128)(4,1)S(1)} %fusion.36, bf16[512,128,1]{1,0,2:T(8,128)(2,1)S(1)} %bitcast.116, bf16[32,256,2,256]{3,1,2,0:T(8,128)(2,1)} %all-to-all-done), kind=kOutput, calls=%fused_computation.10 | convolution fusion | flops 1086324224 | bytes 19015680 | tf_op jit(solution)/shard_map/qd,spd->qsp/dot_general | solution.py:59
  251.9 15.8 %select_reduce_fusion.2 = (f32[512]{0:T(512)S(1)}, f32[512]{0:T(512)S(1)}, f32[32,256,512]{2,1,0:T(8,128)}) fusion(f32[32,256,512]{2,1,0:T(8,128)} %get-tuple-element.20, f32[512]{0:T(512)S(1)} %max.20, pred[32,256]{1,0:T(8,128)(4,1)S(1)} %fusion.36, bf16[512,128,1]{1,0,2:T(8,128)(2,1)S(1)} %bitcast.118, bf16[32,256,2,256]{3,1,2,0:T(8,128)(2,1)} %all-to-all-done), kind=kOutput, calls=%fused_computation.8 | convolution fusion | flops 1103100928 | bytes 35796992 | tf_op jit(solution)/shard_map/qd,spd->qsp/dot_general | solution.py:59
  268.8 7.9 %select_reduce_fusion = f32[512]{0:T(512)S(1)} fusion(f32[32,256,512]{2,1,0:T(8,128)} %get-tuple-element.23, f32[512]{0:T(512)S(1)} %max.22, pred[32,256]{1,0:T(8,128)(4,1)S(1)} %fusion.36), kind=kLoop, calls=%fused_computation.5 | loop fusion | flops 16776704 | bytes 16789504 | tf_op jit(solution)/shard_map/reduce_sum | solution.py:68
  276.7 2.7 copy-done
  279.4 14.0 %fusion.1 = (bf16[512,256,32]{0,1,2:T(8,128)(2,1)}, bf16[512,256,32]{0,1,2:T(8,128)(2,1)}) fusion(f32[32,256,512]{2,1,0:T(8,128)S(1)} %copy-done, f32[512]{0:T(512)S(1)} %max.20, pred[256,32]{0,1:T(8,128)(4,1)S(1)} %fusion.35, f32[512]{0:T(512)S(1)} %max.22, f32[32,256,512]{2,1,0:T(8,128)} %get-tuple-element.23), kind=kLoop, calls=%fused_computation.4 | loop fusion | flops 33554432 | bytes 50343936 | tf_op jit(solution)/shard_map/convert_element_type | solution.py:69
  293.5 14.7 %copy.75 = bf16[512,256,32]{1,2,0:T(8,128)(2,1)} copy(bf16[512,256,32]{0,1,2:T(8,128)(2,1)} %get-tuple-element.15) | data formatting | bytes 16777216 | tf_op jit(solution)/shard_map/convert_element_type | solution.py:69
  308.4 14.8 %copy.86 = bf16[512,256,32]{1,2,0:T(8,128)(2,1)} copy(bf16[512,256,32]{0,1,2:T(8,128)(2,1)} %get-tuple-element.16) | data formatting | bytes 16777216 | tf_op jit(solution)/shard_map/convert_element_type | solution.py:69
  323.3 13.2 %fusion.14 = f32[256,2,128]{0,2,1:T(8,128)S(1)} fusion(bf16[32,256,2,256]{3,1,2,0:T(8,128)(2,1)} %all-to-all-done, bf16[256,2,256,32]{2,3,1,0:T(8,128)(2,1)} %bitcast.110), kind=kOutput, calls=%fused_computation.34 | convolution fusion | flops 1073741824 | bytes 10747904 | tf_op jit(solution)/shard_map/qsp,spd->qd/dot_general | solution.py:72
  337.1 11.1 %fusion.17 = f32[256,2,128]{0,2,1:T(8,128)S(1)} fusion(bf16[32,256,2,256]{3,1,2,0:T(8,128)(2,1)} %all-to-all-done, bf16[256,2,256,32]{2,3,1,0:T(8,128)(2,1)S(1)} %bitcast.109), kind=kOutput, calls=%fused_computation.35 | convolution fusion | flops 1073741824 | bytes 10747904 | tf_op jit(solution)/shard_map/qsp,spd->qd/dot_general | solution.py:72
  348.7 3.8 convolution_convert_fusion
  352.6 41.8 %reduce-scatter.2.cloned.1.call-done = bf16[256,672]{0,1:T(8,128)(2,1)} async-done(((bf16[256,5376]{0,1:T(8,128)(2,1)}), bf16[256,672]{0,1:T(8,128)(2,1)}) %reduce-scatter.2.cloned.1.call-update) | async-done | bytes 344080 | tf_op jit(solution)/shard_map/reduce_scatter | solution.py:147
  (66 shorter events, 5.8 us)
Async XLA Ops:
  49.2 11.3 %copy-start.2 = (bf16[256,2,256]{2,1,0:T(2,128)(2,1)S(1)}, bf16[256,2,256]{2,1,0:T(2,128)(2,1)}, u32[]{:S(2)}) copy-start(bf16[256,2,256]{2,1,0:T(2,128)(2,1)} %param.8) | copy-start | bytes 786436
  49.2 15.3 %copy-start.3 = (bf16[256,512]{1,0:T(8,128)(2,1)S(1)}, bf16[256,512]{1,0:T(8,128)(2,1)}, u32[]{:S(2)}) copy-start(bf16[256,512]{1,0:T(8,128)(2,1)} %param.7) | copy-start | bytes 786436
  49.2 15.5 %copy-start.4 = (s32[16]{0:T(128)S(1)}, s32[16]{0:T(128)}, u32[]{:S(2)}) copy-start(s32[16]{0:T(128)} %param.12) | copy-start | bytes 196
  49.2 15.5 %copy-start.5 = (s32[16]{0:T(128)S(1)}, s32[16]{0:T(128)}, u32[]{:S(2)}) copy-start(s32[16]{0:T(128)} %param.13) | copy-start | bytes 196
  49.3 194.7 %all-to-all-start = ((bf16[32,256,2,256]{3,1,2,0:T(8,128)(2,1)}), bf16[32,256,2,256]{3,1,2,0:T(8,128)(2,1)}, u32[]{:S(2)}, u32[]{:S(2)}) async-start(bf16[32,256,2,256]{3,1,2,0:T(8,128)(2,1)} %copy.67), calls=%async_computation | async-start | bytes 16777216 | tf_op jit(solution)/shard_map/all_to_all | solution.py:112
  60.5 333.9 %reduce-scatter.2.cloned.1.call-start = ((), (), s32[]{:S(2)}) async-start(), calls=%async_computation.2 | async-start | bytes 3096576 | tf_op jit(solution)/shard_map/reduce_scatter | solution.py:147
  60.6 22.1 %collective-permute-start = (bf16[256,2,256]{2,0,1:T(8,128)(2,1)S(1)}, bf16[256,2,256]{2,0,1:T(8,128)(2,1)S(1)}, u32[]{:S(2)}, u32[]{:S(2)}) collective-permute-start(bf16[256,2,256]{2,0,1:T(8,128)(2,1)S(1)} %copy.72), channel_id=1, source_target_pairs={{0,128},{8,136},{16,144},{24,152},{32,160},{40,168},{48,176},{56,1... | collective-permute-start | bytes 786440 | tf_op jit(solution)/shard_map/ppermute | solution.py:15
  268.8 10.6 %copy-start = (f32[32,256,512]{2,1,0:T(8,128)S(1)}, f32[32,256,512]{2,1,0:T(8,128)}, u32[]{:S(2)}) copy-start(f32[32,256,512]{2,1,0:T(8,128)} %get-tuple-element.20) | copy-start | bytes 50331652
  323.3 13.8 %copy-start.1 = (bf16[512,256,32]{1,2,0:T(8,128)(2,1)S(1)}, bf16[512,256,32]{1,2,0:T(8,128)(2,1)}, u32[]{:S(2)}) copy-start(bf16[512,256,32]{1,2,0:T(8,128)(2,1)} %copy.86) | copy-start | bytes 25165828
  336.5 12.2 %slice-start = ((s8[5505024]{0:T(1024)(128)(4,1)}), s8[4194304]{0:T(1024)(128)(4,1)S(1)}, s32[]{:S(2)}) async-start(s8[5505024]{0:T(1024)(128)(4,1)} %bitcast.111), calls=%async_computation.3 | async-start | bytes 8388608
  337.1 11.6 %slice-start.1 = ((s8[5505024]{0:T(1024)(128)(4,1)}), s8[1310720]{0:T(1024)(128)(4,1)S(1)}, s32[]{:S(2)}) async-start(s8[5505024]{0:T(1024)(128)(4,1)} %bitcast.111), calls=%async_computation.4 | async-start | bytes 2621440
Sparse Core Ops, SparseCore 0:
  352.7 41.6 reduce-scatter.1
where the time goes:
time: 410 us; the launch traced here: 402 us
  waiting for transfers between devices  216 us (53%)
  local copies, waits for them, and re-layouts  63 us (15%)
  matrix products  53 us (13%)
  other arithmetic  40.5 us (10%)
  starting transfers between devices  15.2 us (4%)
  between operations  14.3 us (3%)
    all_to_all x1, waiting for transfers between devices, shards(): lax.all_to_all(outgoing, 'seq', split_axis=0, concat_axis=0, tiled=True)  161 us
    reduce_scatter x1, waiting for transfers between devices, shards(): lax.psum_scatter(partial_value.astype(jnp.bfloat16), 'head', scatter_dime...  41.8 us
    convert_element_type x2, local copies, waits for them, and re-layouts, attend(): weights.astype(jnp.bfloat16)  29.5 us
    dot_general x4, matrix products, attend(): jnp.einsum('qsp,spd->qd', rounded, value_rows, preferred_element_type=jnp...  25 us
    dot_general x4, matrix products, attend(): jnp.einsum('qd,spd->qsp', flat_query, key_rows, preferred_element_type=jn...  24.2 us
    gather x1, local copies, waits for them, and re-layouts, pack_pages(): chosen = jnp.take(pooled_pages, chosen_slot, axis=0)  20.6 us
    convert_element_type x1, other arithmetic, attend(): weights.astype(jnp.bfloat16)  14 us
    ppermute x1, waiting for transfers between devices, shifted(): return lax.ppermute(x, axis, pairs)  13.2 us
  transfers between devices with their start and end apart: 3, of which 3 were waited for; matrix products, arithmetic and copies ran while one was open for 1% of the time, Pallas kernels for 0%

commit v1 on v0

v1 whole, which is shorter than its diff:
```python
import functools

import jax
import jax.numpy as jnp
from jax import lax
from jax.experimental import pallas as pl
from jax.experimental.pallas import tpu as pltpu
from jax.sharding import PartitionSpec as P

D = 5376
QUERY_HEADS = 32
KEY_VALUE_HEADS = 16
HEAD_WIDTH = 128
NX, NZ, NY = 4, 8, 4
ROWS = 256
PAGES = 16
NEG = -1e30
SCALE2 = float(D // QUERY_HEADS) ** (-0.5) * 1.4426950408889634
CHIP_COLS = D // NY
WIDE = 1408
DEV_COLS = D // 8
MESH = pl.DeviceIdType.MESH

MESSAGES = (
    ("h", 0, 0), ("h", 1, 0), ("h", 0, 1),
    ("s", 0, 0), ("s", 1, 0), ("s", 3, 0), ("s", 2, 0), ("s", 0, 1),
    ("h", 0, -1), ("h", 1, 1), ("h", 1, -1),
    ("s", 1, 1), ("s", 3, 1), ("s", 0, 2), ("s", 2, 1), ("s", 3, 2),
)
SELF = (0, 3)


def sign(x):
    return 1 - 2 * (x // 2)


def wrap(v, n):
    return lax.rem(v + 4 * n, n)


def home_step(j, dz):
    if j == 0:
        return 0, -dz
    return (-1, 0) if dz == 0 else (1, -dz)


def dest_of(message, x, z):
    kind, a, b = message
    if kind == "h":
        dx, dz = home_step(a, b)
        return wrap(x + dx, NX), wrap(z + dz, NZ)
    to = wrap(x + a, NX)
    return to, wrap(z - sign(to) * b, NZ)


def source_of(message, x, z):
    kind, a, b = message
    if kind == "h":
        dx, dz = home_step(a, b)
        return wrap(x - dx, NX), wrap(z - dz, NZ)
    return wrap(x - a, NX), wrap(z + sign(x) * b, NZ)


def request_of(message, x, z):
    if message[0] == "h":
        return lax.rem(x, 2) * NZ + z
    return lax.rem(x, 2) * NZ + wrap(z - 2 * sign(x), NZ)


def kernel(
    table, suffix_len, q_hbm, skv_hbm, pages_hbm, w_hbm, out_ref,
    pages, sending, kv, skv, q_all, w_all, acc, m_ref, l_ref,
    o_out, o_in, st_out, st_in, attn, total, sib_out, sib_in,
    local_sem, q_send, q_recv, p_send, p_recv, w_send, w_recv,
    o_send, o_recv, t_send, t_recv, a_send, a_recv, b_send, b_recv,
):
    seq = lax.axis_index("seq")
    head = lax.axis_index("head")
    x, z = seq // NZ, lax.rem(seq, NZ)
    y, core = head // 2, lax.rem(head, 2)
    s = sign(x)

    def node(xx, zz):
        return {"seq": xx * NZ + zz, "head": head}

    def chip(dy):
        return {"seq": seq, "head": wrap(y + dy, NY) * 2 + core}

    sibling = {"seq": seq, "head": y * 2 + 1 - core}
    partner = node(wrap(x + 2, NX), z)
    side_near = (x, wrap(z + 2 * s, NZ))
    side_far = (wrap(x + 2, NX), wrap(z - 2 * s, NZ))
    own_side_near = (x, wrap(z - 2 * s, NZ))

    local = [
        pltpu.make_async_copy(pages_hbm, pages, local_sem.at[0]),
        pltpu.make_async_copy(q_hbm, q_all.at[0, 0], local_sem.at[1]),
        pltpu.make_async_copy(skv_hbm, skv, local_sem.at[2]),
    ]
    for copy in local:
        copy.start()

    barrier = pltpu.get_barrier_semaphore()
    heard = 0
    for k, message in enumerate(MESSAGES):
        if k in SELF:
            continue
        pl.semaphore_signal(
            barrier, inc=1, device_id=node(*source_of(message, x, z)), device_id_type=MESH
        )
        heard += 1
    for where in (own_side_near, side_far):
        pl.semaphore_signal(barrier, inc=1, device_id=node(*where), device_id_type=MESH)
        heard += 1
    for dy in (1, 2, 3):
        pl.semaphore_signal(barrier, inc=1, device_id=chip(dy), device_id_type=MESH)
        heard += 1
    pl.semaphore_signal(barrier, inc=1, device_id=sibling, device_id_type=MESH)
    heard += 1

    acc[...] = jnp.zeros_like(acc)
    m_ref[...] = jnp.full(m_ref.shape, NEG, jnp.float32)
    l_ref[...] = jnp.zeros_like(l_ref)
    local[0].wait()
    for k in range(PAGES):
        buffer = kv if k in SELF else sending
        buffer[k] = pages[table[k]]
    pl.semaphore_wait(barrier, heard)

    def remote(src, dst, send, recv, to):
        return pltpu.make_async_remote_copy(
            src_ref=src, dst_ref=dst, send_sem=send, recv_sem=recv,
            device_id=to, device_id_type=MESH,
        )

    q_copies = [
        remote(q_hbm, q_all.at[0, 1], q_send.at[0], q_recv.at[0], partner),
        remote(q_hbm, q_all.at[1, 0], q_send.at[1], q_recv.at[1], node(*side_near)),
        remote(q_hbm, q_all.at[1, 1], q_send.at[2], q_recv.at[2], node(*side_far)),
    ]
    for copy in q_copies:
        copy.start()

    def column(of):
        return pl.multiple_of(((21 * of) // 2) * 128, 128)

    own_weight = pltpu.make_async_copy(
        w_hbm.at[:, pl.ds(column(y), WIDE)], w_all.at[y], local_sem.at[3]
    )
    own_weight.start()
    w_copies = []
    for dy in (1, 3, 2):
        of = wrap(y + dy, NY)
        w_copies.append(
            remote(
                w_hbm.at[:, pl.ds(column(of), WIDE)], w_all.at[y],
                w_send.at[dy - 1], w_recv.at[dy - 1], chip(dy),
            )
        )
        w_copies[-1].start()

    p_copies = []
    for k, message in enumerate(MESSAGES):
        if k in SELF:
            continue
        copy = remote(
            sending.at[k], kv.at[k], p_send.at[k], p_recv.at[k],
            node(*dest_of(message, x, z)),
        )
        copy.start()
        p_copies.append(copy)

    rows = lax.broadcasted_iota(jnp.int32, (ROWS, ROWS), 0)
    cols = lax.broadcasted_iota(jnp.int32, (ROWS, ROWS), 1)

    def attend(st, block, masks, members=(0, 1)):
        for g in range(2):
            lanes = slice(g * HEAD_WIDTH, (g + 1) * HEAD_WIDTH)
            keys = block[:, 0, lanes]
            values = block[:, 1, lanes].T
            for mi in members:
                for u in range(2):
                    first = (2 * g + u) * HEAD_WIDTH
                    query = q_all[st, mi, :, first:first + HEAD_WIDTH]
                    c = (g * 2 + mi) * 2 + u
                    scores = lax.dot_general(
                        keys, query, (((1,), (1,)), ((), ())),
                        preferred_element_type=jnp.float32,
                    )
                    scores = jnp.where(masks[mi], scores, NEG)
                    old = m_ref[st, c:c + 1, :]
                    new = jnp.maximum(old, jnp.max(scores, axis=0, keepdims=True))
                    weights = jnp.exp2((scores - new) * SCALE2)
                    keep = jnp.exp2((old - new) * SCALE2)
                    m_ref[st, c:c + 1, :] = new
                    l_ref[st, c:c + 1, :] = l_ref[st, c:c + 1, :] * keep + jnp.sum(
                        weights, axis=0, keepdims=True
                    )
                    mixed = jnp.dot(
                        values, weights.astype(jnp.bfloat16),
                        preferred_element_type=jnp.float32,
                    )
                    acc[st, c] = acc[st, c] * keep + mixed

    member = x // 2
    mine = suffix_len[lax.rem(x, 2) * NZ + z]
    here = mine - member * ROWS
    local[1].wait()
    local[2].wait()
    q_copies[0].wait_recv()
    attend(
        0, skv,
        {0: (rows <= cols) & (rows < here), 1: rows < here * (1 - member)},
    )
    q_copies[1].wait_recv()
    q_copies[2].wait_recv()

    def step(i, carry):
        st = (lax.rem(i, 8) + 5) // 8

        @pl.when((i != SELF[0]) & (i != SELF[1]))
        def _():
            remote(
                sending.at[i], kv.at[i], p_send.at[i], p_recv.at[i], partner
            ).wait_recv()

        mask = rows < table[PAGES + i]
        attend(st, kv.at[i], {0: mask, 1: mask})
        return carry

    lax.fori_loop(0, PAGES, step, 0)

    targets = ((0, 1, partner), (1, 0, node(*own_side_near)), (1, 1, node(*side_far)))
    o_copies = {}
    for g in range(2):
        for n, (st, mi, to) in enumerate(targets):
            for u in range(2):
                c = (g * 2 + mi) * 2 + u
                share = l_ref[st, c:c + 1, :]
                o_out[g, n, u] = (acc[st, c] / share).astype(jnp.bfloat16)
                st_out[g, n, u:u + 1, :] = m_ref[st, c:c + 1, :]
                st_out[g, n, 2 + u:3 + u, :] = share
            e = g * 3 + n
            pair = (
                remote(st_out.at[g, n], st_in.at[g, n], t_send.at[e], t_recv.at[e], to),
                remote(o_out.at[g, n], o_in.at[g, n], o_send.at[e], o_recv.at[e], to),
            )
            for copy in pair:
                copy.start()
            o_copies[g, n] = pair

    a_copies = {}
    live = lax.broadcasted_iota(jnp.int32, (1, ROWS), 1) < here
    for g in range(2):
        for n in range(3):
            for copy in o_copies[g, n]:
                copy.wait_recv()
        for u in range(2):
            c = g * 4 + u
            tops = [m_ref[0, c:c + 1, :]] + [st_in[g, n, u:u + 1, :] for n in range(3)]
            sums = [l_ref[0, c:c + 1, :]] + [st_in[g, n, 2 + u:3 + u, :] for n in range(3)]
            top = jnp.maximum(jnp.maximum(tops[0], tops[1]), jnp.maximum(tops[2], tops[3]))
            factors = [jnp.exp2((t - top) * SCALE2) for t in tops]
            shares = [f * l for f, l in zip(factors, sums)]
            whole = shares[0] + shares[1] + shares[2] + shares[3]
            inverse = jnp.where(live, 1.0 / whole, 0.0)
            value = acc[0, c] * (factors[0] * inverse)
            for n in range(3):
                value += o_in[g, n, u].astype(jnp.float32) * (shares[n + 1] * inverse)
            first = (2 * g + u) * HEAD_WIDTH
            attn[y, :, first:first + HEAD_WIDTH] = value.T.astype(jnp.bfloat16)
        half = pl.ds(g * 256, 256)
        for dy in (1, 3, 2):
            e = g * 3 + dy - 1
            copy = remote(
                attn.at[y, :, half], attn.at[y, :, half], a_send.at[e], a_recv.at[e], chip(dy)
            )
            copy.start()
            a_copies[g, dy] = copy

    own_weight.wait()
    total[...] = jnp.dot(attn[y], w_all[y], preferred_element_type=jnp.float32)
    for n, dy in enumerate((1, 3, 2)):
        w_copies[n].wait_recv()
    for g in range(2):
        for dy in (1, 3, 2):
            a_copies[g, dy].wait_recv()
            of = wrap(y - dy, NY)
            total[...] += jnp.dot(
                attn[of, :, g * 256:(g + 1) * 256], w_all[of, g * 256:(g + 1) * 256, :],
                preferred_element_type=jnp.float32,
            )

    def columns_of(c):
        return pltpu.roll(total[...], WIDE - 64 * lax.rem(y, 2) - DEV_COLS * c, 1)[:, :768]

    sib_out[...] = columns_of(1 - core).astype(jnp.bfloat16)
    swap = remote(sib_out, sib_in, b_send.at[0], b_recv.at[0], sibling)
    swap.start()
    own = columns_of(core)
    swap.wait_recv()
    out_ref[...] = (own + sib_in[...].astype(jnp.float32)).astype(jnp.bfloat16)[:, :DEV_COLS]

    for copy in q_copies + w_copies + p_copies + list(a_copies.values()) + [swap]:
        copy.wait_send()
    for pair in o_copies.values():
        for copy in pair:
            copy.wait_send()


def shards(queries, suffix_key_value, pooled_pages, out_weight, page_table, prefix_len, suffix_len):
    seq = lax.axis_index("seq")
    x, z = seq // NZ, lax.rem(seq, NZ)
    devices, requests = [], []
    for message in MESSAGES:
        devices.append(seq)
        requests.append(request_of(message, *dest_of(message, x, z)))
    for message in MESSAGES:
        xx, zz = source_of(message, x, z)
        devices.append(xx * NZ + zz)
        requests.append(request_of(message, x, z))
    devices = jnp.stack(devices)[:, None, None]
    requests = jnp.stack(requests)[:, None, None]
    request = jnp.arange(page_table.shape[0], dtype=jnp.int32)[None, :, None]
    position = jnp.arange(page_table.shape[1], dtype=jnp.int32)[None, None, :] * ROWS
    entry = jnp.arange(2 * PAGES, dtype=jnp.int32)[:, None, None]
    chosen = (request == requests) & (page_table[None] // PAGES == devices)
    value = jnp.where(
        entry < PAGES, page_table[None] % PAGES, prefix_len[None, :, None] - position
    )
    table = jnp.sum(jnp.where(chosen, value, 0), axis=(1, 2))

    vmem = pltpu.VMEM
    dma = pltpu.SemaphoreType.DMA
    bf16, f32 = jnp.bfloat16, jnp.float32
    return pl.pallas_call(
        kernel,
        out_shape=jax.ShapeDtypeStruct((ROWS, DEV_COLS), bf16),
        in_specs=[pl.BlockSpec(memory_space=pltpu.SMEM)] * 2
        + [pl.BlockSpec(memory_space=pl.ANY)] * 4,
        out_specs=pl.BlockSpec(memory_space=vmem),
        scratch_shapes=[
            vmem((PAGES, ROWS, 2, 256), bf16),
            vmem((PAGES, ROWS, 2, 256), bf16),
            vmem((PAGES, ROWS, 2, 256), bf16),
            vmem((ROWS, 2, 256), bf16),
            vmem((2, 2, ROWS, 512), bf16),
            vmem((NY, 512, WIDE), bf16),
            vmem((2, 8, HEAD_WIDTH, ROWS), f32),
            vmem((2, 8, ROWS), f32),
            vmem((2, 8, ROWS), f32),
            vmem((2, 3, 2, HEAD_WIDTH, ROWS), bf16),
            vmem((2, 3, 2, HEAD_WIDTH, ROWS), bf16),
            vmem((2, 3, 8, ROWS), f32),
            vmem((2, 3, 8, ROWS), f32),
            vmem((NY, ROWS, 512), bf16),
            vmem((ROWS, WIDE), f32),
            vmem((ROWS, 768), bf16),
            vmem((ROWS, 768), bf16),
            dma((4,)), dma((3,)), dma((3,)), dma((PAGES,)), dma((PAGES,)), dma((3,)), dma((3,)),
            dma((6,)), dma((6,)), dma((6,)), dma((6,)), dma((6,)), dma((6,)), dma((1,)), dma((1,)),
        ],
        compiler_params=pltpu.CompilerParams(
            collective_id=0, has_side_effects=True, vmem_limit_bytes=56 * 1024 * 1024
        ),
        name="paged_prefill",
    )(table, suffix_len, queries, suffix_key_value, pooled_pages, out_weight)


def solution(mesh):
    placed = (
        P("seq", "head"),
        P("seq", None, "head"),
        P("seq", None, None, "head"),
        P("head", None),
        P(),
        P(),
        P(),
    )
    return jax.shard_map(
        shards, mesh=mesh, in_specs=placed, out_specs=P("seq", "head"), check_vma=False
    )
```

time: 410 us -> 129 us (0.31)
  the two profiles are of different devices: /device:TPU:3 before, /device:TPU:33 now
where the time goes in v1:
time: 129 us
  Pallas kernels  125 us (97%)
  other arithmetic  2.21 us (2%)
  local copies, waits for them, and re-layouts  2.12 us (2%)
    pallas_call x1, Pallas kernels, shards(): pl.pallas_call(kernel, out_shape=jax.ShapeDtypeStruct((ROWS, DEV_COLS), b...  125 us

profile of v1, /device:TPU:33, one launch (start us, length us, event | category | flops | bytes accessed | tf_op | source)
XLA Modules:
  0.0 129.2 jit_solution(4164946556869642077)
XLA Ops:
  0.0 0.1 stack.156
  0.1 0.1 stack.173
  0.2 0.1 iota_compare_fusion
  0.3 0.8 add_select_fusion.1
  1.1 1.4 %select_reduce_fusion.table = s32[32]{0:T(128)} fusion(s32[16,32]{1,0:T(8,128)S(1)} %get-tuple-element.7, s32[16,32]{1,0:T(8,128)S(1)} %get-tuple-element.6, s32[16,32]{1,0:T(8,128)S(1)} %get-tuple-element.5, s32[32]{0:T(128)S(1)} %stack.173, pred[32]{0:T(512)(128)(4,1)S(1)} %iota_compare_fusion.1, pred[32,16]{1,0:T(8,128)(4,1)S(1)} %iota_compare_fusion), kind=kLoop, calls=%fused_computation | loop fusion | flops 81888 | bytes 6944 | tf_op jit(solution)/shard_map/reduce_sum | solution.py:331
  2.5 124.8 %paged_prefill.1 = bf16[256,672]{1,0:T(8,128)(2,1)} custom-call(s32[32]{0:T(128)} %select_reduce_fusion.table, s32[16]{0:T(128)} %suffix_len.1, bf16[256,512]{1,0:T(8,128)(2,1)} %q_hbm.1, bf16[256,2,256]{2,1,0:T(2,128)(2,1)} %skv_hbm.1, bf16[16,256,2,256]{3,2,1,0:T(2,128)(2,1)} %pages_hbm.1, bf16[512,5376]{1,0:T(8,128)(2,1)} %w_hbm.1), custom_call_target="tpu_custom_call" | custom-call | tf_op jit(solution)/shard_map/paged_prefill/pallas_call | solution.py:336
  127.3 1.9 %copy.9 = bf16[256,672]{0,1:T(8,128)(2,1)} copy(bf16[256,672]{1,0:T(8,128)(2,1)} %paged_prefill.1) | data formatting | bytes 688128 | tf_op jit(solution)/shard_map/paged_prefill/pallas_call | solution.py:336
  (2 shorter events, 0.0 us)

commit v2 on v1

--- a/solution.py
+++ b/solution.py
@@ -22,16 +22,17 @@
 MESH = pl.DeviceIdType.MESH
 
 MESSAGES = (
-    ("h", 0, 0), ("h", 1, 0), ("h", 0, 1),
-    ("s", 0, 0), ("s", 1, 0), ("s", 3, 0), ("s", 2, 0), ("s", 0, 1),
-    ("h", 0, -1), ("h", 1, 1), ("h", 1, -1),
-    ("s", 1, 1), ("s", 3, 1), ("s", 0, 2), ("s", 2, 1), ("s", 3, 2),
+    ("h", 0, 0), ("s", 0, 0),
+    ("s", 1, 0), ("s", 3, 0), ("s", 0, 1), ("s", 2, 0), ("s", 0, 2),
+    ("s", 1, 1), ("s", 3, 1), ("s", 3, 2), ("s", 2, 1),
+    ("h", 0, 1), ("h", 0, -1), ("h", 1, 0), ("h", 1, 1), ("h", 1, -1),
 )
-SELF = (0, 3)
-
-
-def sign(x):
-    return 1 - 2 * (x // 2)
+SELF = (0, 1)
+SIDE_END = 11
+
+
+def sign(x, z):
+    return 1 - 2 * lax.rem(x // 2 + z, 2)
 
 
 def wrap(v, n):
@@ -50,7 +51,7 @@
         dx, dz = home_step(a, b)
         return wrap(x + dx, NX), wrap(z + dz, NZ)
     to = wrap(x + a, NX)
-    return to, wrap(z - sign(to) * b, NZ)
+    return to, wrap(z - sign(to, z + b) * b, NZ)
 
 
 def source_of(message, x, z):
@@ -58,13 +59,13 @@
     if kind == "h":
         dx, dz = home_step(a, b)
         return wrap(x - dx, NX), wrap(z - dz, NZ)
-    return wrap(x - a, NX), wrap(z + sign(x) * b, NZ)
+    return wrap(x - a, NX), wrap(z + sign(x, z) * b, NZ)
 
 
 def request_of(message, x, z):
     if message[0] == "h":
         return lax.rem(x, 2) * NZ + z
-    return lax.rem(x, 2) * NZ + wrap(z - 2 * sign(x), NZ)
+    return lax.rem(x, 2) * NZ + wrap(z - 2 * sign(x, z), NZ)
 
 
 def kernel(
@@ -78,7 +79,7 @@
     head = lax.axis_index("head")
     x, z = seq // NZ, lax.rem(seq, NZ)
     y, core = head // 2, lax.rem(head, 2)
-    s = sign(x)
+    s = sign(x, z)
 
     def node(xx, zz):
         return {"seq": xx * NZ + zz, "head": head}
@@ -212,28 +213,25 @@
         0, skv,
         {0: (rows <= cols) & (rows < here), 1: rows < here * (1 - member)},
     )
-    q_copies[1].wait_recv()
-    q_copies[2].wait_recv()
-
-    def step(i, carry):
-        st = (lax.rem(i, 8) + 5) // 8
-
-        @pl.when((i != SELF[0]) & (i != SELF[1]))
-        def _():
+    def unit(st, i, received):
+        if received:
             remote(
                 sending.at[i], kv.at[i], p_send.at[i], p_recv.at[i], partner
             ).wait_recv()
-
         mask = rows < table[PAGES + i]
         attend(st, kv.at[i], {0: mask, 1: mask})
-        return carry
-
-    lax.fori_loop(0, PAGES, step, 0)
+
+    unit(0, SELF[0], False)
+    q_copies[1].wait_recv()
+    q_copies[2].wait_recv()
+    unit(1, SELF[1], False)
 
     targets = ((0, 1, partner), (1, 0, node(*own_side_near)), (1, 1, node(*side_far)))
     o_copies = {}
-    for g in range(2):
-        for n, (st, mi, to) in enumerate(targets):
+
+    def give(n):
+        st, mi, to = targets[n]
+        for g in range(2):
             for u in range(2):
                 c = (g * 2 + mi) * 2 + u
                 share = l_ref[st, c:c + 1, :]
@@ -248,6 +246,20 @@
             for copy in pair:
                 copy.start()
             o_copies[g, n] = pair
+
+    def side_unit(i, carry):
+        unit(1, i, True)
+        return carry
+
+    def home_unit(i, carry):
+        unit(0, i, True)
+        return carry
+
+    lax.fori_loop(2, SIDE_END, side_unit, 0)
+    give(2)
+    give(1)
+    lax.fori_loop(SIDE_END, PAGES, home_unit, 0)
+    give(0)
 
     a_copies = {}
     live = lax.broadcasted_iota(jnp.int32, (1, ROWS), 1) < here

time: 129 us -> 115 us (0.89)
  the two profiles are of different devices: /device:TPU:33 before, /device:TPU:3 now
where the time goes in v2:
time: 115 us
  Pallas kernels  110 us (96%)
  other arithmetic  2.21 us (2%)
  local copies, waits for them, and re-layouts  2.12 us (2%)
    pallas_call x1, Pallas kernels, shards(): pl.pallas_call(kernel, out_shape=jax.ShapeDtypeStruct((ROWS, DEV_COLS), b...  110 us

profile of v2, /device:TPU:3, one launch (start us, length us, event | category | flops | bytes accessed | tf_op | source)
XLA Modules:
  0.0 114.6 jit_solution(16743825459649221189)
XLA Ops:
  0.0 0.1 stack.156
  0.1 0.1 stack.173
  0.2 0.1 iota_compare_fusion
  0.3 0.8 add_select_fusion.1
  1.1 1.4 %select_reduce_fusion.table = s32[32]{0:T(128)} fusion(s32[16,32]{1,0:T(8,128)S(1)} %get-tuple-element.7, s32[16,32]{1,0:T(8,128)S(1)} %get-tuple-element.6, s32[16,32]{1,0:T(8,128)S(1)} %get-tuple-element.5, s32[32]{0:T(128)S(1)} %stack.173, pred[32]{0:T(512)(128)(4,1)S(1)} %iota_compare_fusion.1, pred[32,16]{1,0:T(8,128)(4,1)S(1)} %iota_compare_fusion), kind=kLoop, calls=%fused_computation | loop fusion | flops 81888 | bytes 6944 | tf_op jit(solution)/shard_map/reduce_sum | solution.py:343
  2.5 110.2 %paged_prefill.1 = bf16[256,672]{1,0:T(8,128)(2,1)} custom-call(s32[32]{0:T(128)} %select_reduce_fusion.table, s32[16]{0:T(128)} %suffix_len.1, bf16[256,512]{1,0:T(8,128)(2,1)} %q_hbm.1, bf16[256,2,256]{2,1,0:T(2,128)(2,1)} %skv_hbm.1, bf16[16,256,2,256]{3,2,1,0:T(2,128)(2,1)} %pages_hbm.1, bf16[512,5376]{1,0:T(8,128)(2,1)} %w_hbm.1), custom_call_target="tpu_custom_call" | custom-call | tf_op jit(solution)/shard_map/paged_prefill/pallas_call | solution.py:348
  112.7 1.9 %copy.9 = bf16[256,672]{0,1:T(8,128)(2,1)} copy(bf16[256,672]{1,0:T(8,128)(2,1)} %paged_prefill.1) | data formatting | bytes 688128 | tf_op jit(solution)/shard_map/paged_prefill/pallas_call | solution.py:348
  (2 shorter events, 0.0 us)

commit v3 on v2

--- a/solution.py
+++ b/solution.py
@@ -69,9 +69,9 @@
 
 
 def kernel(
-    table, suffix_len, q_hbm, skv_hbm, pages_hbm, w_hbm, out_ref,
+    owners, prefix_len, suffix_len, q_hbm, skv_hbm, pages_hbm, w_hbm, out_ref,
     pages, sending, kv, skv, q_all, w_all, acc, m_ref, l_ref,
-    o_out, o_in, st_out, st_in, attn, total, sib_out, sib_in,
+    o_out, o_in, st_out, st_in, attn, total, turned, sib_out, sib_in, slots, counts,
     local_sem, q_send, q_recv, p_send, p_recv, w_send, w_recv,
     o_send, o_recv, t_send, t_recv, a_send, a_recv, b_send, b_recv,
 ):
@@ -122,10 +122,32 @@
     acc[...] = jnp.zeros_like(acc)
     m_ref[...] = jnp.full(m_ref.shape, NEG, jnp.float32)
     l_ref[...] = jnp.zeros_like(l_ref)
+    place = lax.broadcasted_iota(jnp.int32, (1, owners.shape[1]), 1) * ROWS
+    for k, message in enumerate(MESSAGES):
+        row = owners[pl.ds(request_of(message, *dest_of(message, x, z)), 1), :]
+        slots[k] = jnp.sum(
+            jnp.where(jnp.right_shift(row, 4) == seq, jnp.bitwise_and(row, PAGES - 1), 0)
+        )
+        served = request_of(message, x, z)
+        xx, zz = source_of(message, x, z)
+        row = owners[pl.ds(served, 1), :]
+        counts[k] = jnp.sum(
+            jnp.where(jnp.right_shift(row, 4) == xx * NZ + zz, prefix_len[served] - place, 0)
+        )
     local[0].wait()
-    for k in range(PAGES):
-        buffer = kv if k in SELF else sending
-        buffer[k] = pages[table[k]]
+
+    def split(page, block):
+        block[0] = page[:, 0, :]
+        block[1] = page[:, 1, :].T
+
+    def stage(first, last, buffer):
+        def one(k, carry):
+            split(pages[slots[k]], buffer.at[k])
+            return carry
+
+        lax.fori_loop(first, last, one, 0)
+
+    stage(2, 6, sending)
     pl.semaphore_wait(barrier, heard)
 
     def remote(src, dst, send, recv, to):
@@ -164,6 +186,10 @@
     for k, message in enumerate(MESSAGES):
         if k in SELF:
             continue
+        if k == 6:
+            stage(6, SIDE_END, sending)
+        if k == SIDE_END:
+            stage(SIDE_END, PAGES, sending)
         copy = remote(
             sending.at[k], kv.at[k], p_send.at[k], p_recv.at[k],
             node(*dest_of(message, x, z)),
@@ -177,8 +203,8 @@
     def attend(st, block, masks, members=(0, 1)):
         for g in range(2):
             lanes = slice(g * HEAD_WIDTH, (g + 1) * HEAD_WIDTH)
-            keys = block[:, 0, lanes]
-            values = block[:, 1, lanes].T
+            keys = block[0, :, lanes]
+            values = block[1, lanes, :]
             for mi in members:
                 for u in range(2):
                     first = (2 * g + u) * HEAD_WIDTH
@@ -206,25 +232,28 @@
     member = x // 2
     mine = suffix_len[lax.rem(x, 2) * NZ + z]
     here = mine - member * ROWS
+    stage(0, 2, kv)
+    local[2].wait()
+    split(skv[...], kv.at[PAGES])
     local[1].wait()
-    local[2].wait()
+    own_mask = rows < counts[0]
+    attend(0, kv.at[PAGES], {0: (rows <= cols) & (rows < here)}, (0,))
+    attend(0, kv.at[0], {0: own_mask}, (0,))
     q_copies[0].wait_recv()
-    attend(
-        0, skv,
-        {0: (rows <= cols) & (rows < here), 1: rows < here * (1 - member)},
-    )
-    def unit(st, i, received):
-        if received:
+    attend(0, kv.at[PAGES], {1: rows < here * (1 - member)}, (1,))
+    attend(0, kv.at[0], {1: own_mask}, (1,))
+    def unit(st, i):
+        @pl.when(i != SELF[1])
+        def _():
             remote(
                 sending.at[i], kv.at[i], p_send.at[i], p_recv.at[i], partner
             ).wait_recv()
-        mask = rows < table[PAGES + i]
+
+        mask = rows < counts[i]
         attend(st, kv.at[i], {0: mask, 1: mask})
 
-    unit(0, SELF[0], False)
     q_copies[1].wait_recv()
     q_copies[2].wait_recv()
-    unit(1, SELF[1], False)
 
     targets = ((0, 1, partner), (1, 0, node(*own_side_near)), (1, 1, node(*side_far)))
     o_copies = {}
@@ -235,7 +264,7 @@
             for u in range(2):
                 c = (g * 2 + mi) * 2 + u
                 share = l_ref[st, c:c + 1, :]
-                o_out[g, n, u] = (acc[st, c] / share).astype(jnp.bfloat16)
+                o_out[g, n, u] = (acc[st, c] * (1.0 / share)).astype(jnp.bfloat16)
                 st_out[g, n, u:u + 1, :] = m_ref[st, c:c + 1, :]
                 st_out[g, n, 2 + u:3 + u, :] = share
             e = g * 3 + n
@@ -248,14 +277,14 @@
             o_copies[g, n] = pair
 
     def side_unit(i, carry):
-        unit(1, i, True)
+        unit(1, i)
         return carry
 
     def home_unit(i, carry):
-        unit(0, i, True)
+        unit(0, i)
         return carry
 
-    lax.fori_loop(2, SIDE_END, side_unit, 0)
+    lax.fori_loop(SELF[1], SIDE_END, side_unit, 0)
     give(2)
     give(1)
     lax.fori_loop(SIDE_END, PAGES, home_unit, 0)
@@ -303,15 +332,18 @@
                 preferred_element_type=jnp.float32,
             )
 
+    turned[...] = total[...].T
+
     def columns_of(c):
-        return pltpu.roll(total[...], WIDE - 64 * lax.rem(y, 2) - DEV_COLS * c, 1)[:, :768]
+        first = 64 * lax.rem(y, 2) + DEV_COLS * c
+        return turned[pl.ds(pl.multiple_of(first, 32), DEV_COLS), :]
 
     sib_out[...] = columns_of(1 - core).astype(jnp.bfloat16)
     swap = remote(sib_out, sib_in, b_send.at[0], b_recv.at[0], sibling)
     swap.start()
     own = columns_of(core)
     swap.wait_recv()
-    out_ref[...] = (own + sib_in[...].astype(jnp.float32)).astype(jnp.bfloat16)[:, :DEV_COLS]
+    out_ref[...] = (own + sib_in[...].astype(jnp.float32)).astype(jnp.bfloat16)
 
     for copy in q_copies + w_copies + p_copies + list(a_copies.values()) + [swap]:
         copy.wait_send()
@@ -321,40 +353,20 @@
 
 
 def shards(queries, suffix_key_value, pooled_pages, out_weight, page_table, prefix_len, suffix_len):
-    seq = lax.axis_index("seq")
-    x, z = seq // NZ, lax.rem(seq, NZ)
-    devices, requests = [], []
-    for message in MESSAGES:
-        devices.append(seq)
-        requests.append(request_of(message, *dest_of(message, x, z)))
-    for message in MESSAGES:
-        xx, zz = source_of(message, x, z)
-        devices.append(xx * NZ + zz)
-        requests.append(request_of(message, x, z))
-    devices = jnp.stack(devices)[:, None, None]
-    requests = jnp.stack(requests)[:, None, None]
-    request = jnp.arange(page_table.shape[0], dtype=jnp.int32)[None, :, None]
-    position = jnp.arange(page_table.shape[1], dtype=jnp.int32)[None, None, :] * ROWS
-    entry = jnp.arange(2 * PAGES, dtype=jnp.int32)[:, None, None]
-    chosen = (request == requests) & (page_table[None] // PAGES == devices)
-    value = jnp.where(
-        entry < PAGES, page_table[None] % PAGES, prefix_len[None, :, None] - position
-    )
-    table = jnp.sum(jnp.where(chosen, value, 0), axis=(1, 2))
-
     vmem = pltpu.VMEM
     dma = pltpu.SemaphoreType.DMA
     bf16, f32 = jnp.bfloat16, jnp.float32
     return pl.pallas_call(
         kernel,
-        out_shape=jax.ShapeDtypeStruct((ROWS, DEV_COLS), bf16),
-        in_specs=[pl.BlockSpec(memory_space=pltpu.SMEM)] * 2
+        out_shape=jax.ShapeDtypeStruct((DEV_COLS, ROWS), bf16),
+        in_specs=[pl.BlockSpec(memory_space=vmem)]
+        + [pl.BlockSpec(memory_space=pltpu.SMEM)] * 2
         + [pl.BlockSpec(memory_space=pl.ANY)] * 4,
         out_specs=pl.BlockSpec(memory_space=vmem),
         scratch_shapes=[
             vmem((PAGES, ROWS, 2, 256), bf16),
-            vmem((PAGES, ROWS, 2, 256), bf16),
-            vmem((PAGES, ROWS, 2, 256), bf16),
+            vmem((PAGES, 2, ROWS, 256), bf16),
+            vmem((PAGES + 1, 2, ROWS, 256), bf16),
             vmem((ROWS, 2, 256), bf16),
             vmem((2, 2, ROWS, 512), bf16),
             vmem((NY, 512, WIDE), bf16),
@@ -367,8 +379,11 @@
             vmem((2, 3, 8, ROWS), f32),
             vmem((NY, ROWS, 512), bf16),
             vmem((ROWS, WIDE), f32),
-            vmem((ROWS, 768), bf16),
-            vmem((ROWS, 768), bf16),
+            vmem((WIDE, ROWS), f32),
+            vmem((DEV_COLS, ROWS), bf16),
+            vmem((DEV_COLS, ROWS), bf16),
+            pltpu.SMEM((PAGES,), jnp.int32),
+            pltpu.SMEM((PAGES,), jnp.int32),
             dma((4,)), dma((3,)), dma((3,)), dma((PAGES,)), dma((PAGES,)), dma((3,)), dma((3,)),
             dma((6,)), dma((6,)), dma((6,)), dma((6,)), dma((6,)), dma((6,)), dma((1,)), dma((1,)),
         ],
@@ -376,7 +391,9 @@
             collective_id=0, has_side_effects=True, vmem_limit_bytes=56 * 1024 * 1024
         ),
         name="paged_prefill",
-    )(table, suffix_len, queries, suffix_key_value, pooled_pages, out_weight)
+    )(
+        page_table, prefix_len, suffix_len, queries, suffix_key_value, pooled_pages, out_weight
+    ).T
 
 
 def solution(mesh):

time: 115 us -> 109 us (0.948)
  Pallas kernels: 110 us -> 107 us
  other arithmetic: 2.21 us -> 0 us
    pallas_call x1, Pallas kernels: 110 us -> 107 us  [shards(): pl.pallas_call(kernel, out_shape=jax.ShapeDtypeStruct((DEV_COLS, ROWS), b...]
    pallas_call x1 -> x0, local copies, waits for them, and re-layouts: 1.9 us -> none  [shards(): pl.pallas_call(kernel, out_shape=jax.ShapeDtypeStruct((ROWS, DEV_COLS), b...]
    unnamed x0 -> x1, local copies, waits for them, and re-layouts: none -> 1.73 us
    reduce_sum x1 -> x0, other arithmetic: 1.36 us -> none  [shards(): table = jnp.sum(jnp.where(chosen, value, 0), axis=(1, 2))]
where the time goes in v3:
time: 109 us
  Pallas kernels  107 us (98%)
  local copies, waits for them, and re-layouts  1.73 us (2%)
    pallas_call x1, Pallas kernels, shards(): pl.pallas_call(kernel, out_shape=jax.ShapeDtypeStruct((DEV_COLS, ROWS), b...  107 us

profile of v3, /device:TPU:3, one launch (start us, length us, event | category | flops | bytes accessed | tf_op | source)
XLA Modules:
  0.0 108.5 jit_solution(1343003497676529135)
XLA Ops:
  0.0 106.8 %paged_prefill.1 = bf16[672,256]{1,0:T(8,128)(2,1)} custom-call(s32[16,32]{1,0:T(8,128)} %owners.1, s32[16]{0:T(128)} %prefix_len.1, s32[16]{0:T(128)} %suffix_len.1, bf16[256,512]{1,0:T(8,128)(2,1)} %q_hbm.1, bf16[256,2,256]{2,1,0:T(2,128)(2,1)} %skv_hbm.1, bf16[16,256,2,256]{3,2,1,0:T(2,128)(2,1)} %pages_hbm.1, bf16[512,5376]{1,0:T(8,128)(2,1)} %w_hbm.1), custom_call_target="tpu_custom_call" | custom-call | tf_op jit(solution)/shard_map/paged_prefill/pallas_call | solution.py:359
  106.8 1.7 %copy.9 = bf16[256,672]{0,1:T(8,128)(2,1)} copy(bf16[256,672]{0,1:T(8,128)(2,1)} %bitcast.1) | data formatting | bytes 688128

commit v4 on v3

--- a/solution.py
+++ b/solution.py
@@ -23,12 +23,14 @@
 
 MESSAGES = (
     ("h", 0, 0), ("s", 0, 0),
-    ("s", 1, 0), ("s", 3, 0), ("s", 0, 1), ("s", 2, 0), ("s", 0, 2),
-    ("s", 1, 1), ("s", 3, 1), ("s", 3, 2), ("s", 2, 1),
-    ("h", 0, 1), ("h", 0, -1), ("h", 1, 0), ("h", 1, 1), ("h", 1, -1),
+    ("s", 0, 2), ("s", 2, 0), ("s", 2, 1), ("s", 3, 2), ("s", 1, 1),
+    ("s", 3, 1), ("s", 0, 1), ("s", 1, 0), ("s", 3, 0),
+    ("h", 1, 1), ("h", 1, -1), ("h", 1, 0), ("h", 0, 1), ("h", 0, -1),
 )
 SELF = (0, 1)
 SIDE_END = 11
+FLIGHT = 8
+EARLY = 3
 
 
 def sign(x, z):
@@ -184,18 +186,18 @@
 
     p_copies = []
     for k, message in enumerate(MESSAGES):
-        if k in SELF:
-            continue
-        if k == 6:
-            stage(6, SIDE_END, sending)
-        if k == SIDE_END:
-            stage(SIDE_END, PAGES, sending)
-        copy = remote(
-            sending.at[k], kv.at[k], p_send.at[k], p_recv.at[k],
-            node(*dest_of(message, x, z)),
-        )
-        copy.start()
-        p_copies.append(copy)
+        p_copies.append(
+            remote(
+                sending.at[k], kv.at[k], p_send.at[k], p_recv.at[k],
+                node(*dest_of(message, x, z)),
+            )
+        )
+    for k in range(2, 2 + EARLY):
+        p_copies[k].start()
+    stage(6, SIDE_END, sending)
+    stage(SIDE_END, PAGES, sending)
+    for k in range(2 + EARLY, 2 + FLIGHT):
+        p_copies[k].start()
 
     rows = lax.broadcasted_iota(jnp.int32, (ROWS, ROWS), 0)
     cols = lax.broadcasted_iota(jnp.int32, (ROWS, ROWS), 1)
@@ -205,29 +207,32 @@
             lanes = slice(g * HEAD_WIDTH, (g + 1) * HEAD_WIDTH)
             keys = block[0, :, lanes]
             values = block[1, lanes, :]
-            for mi in members:
-                for u in range(2):
-                    first = (2 * g + u) * HEAD_WIDTH
-                    query = q_all[st, mi, :, first:first + HEAD_WIDTH]
-                    c = (g * 2 + mi) * 2 + u
-                    scores = lax.dot_general(
-                        keys, query, (((1,), (1,)), ((), ())),
-                        preferred_element_type=jnp.float32,
-                    )
-                    scores = jnp.where(masks[mi], scores, NEG)
-                    old = m_ref[st, c:c + 1, :]
-                    new = jnp.maximum(old, jnp.max(scores, axis=0, keepdims=True))
-                    weights = jnp.exp2((scores - new) * SCALE2)
-                    keep = jnp.exp2((old - new) * SCALE2)
-                    m_ref[st, c:c + 1, :] = new
-                    l_ref[st, c:c + 1, :] = l_ref[st, c:c + 1, :] * keep + jnp.sum(
-                        weights, axis=0, keepdims=True
-                    )
-                    mixed = jnp.dot(
-                        values, weights.astype(jnp.bfloat16),
-                        preferred_element_type=jnp.float32,
-                    )
-                    acc[st, c] = acc[st, c] * keep + mixed
+            parts = [(mi, u) for mi in members for u in range(2)]
+            scores, olds = [], []
+            for mi, u in parts:
+                first = (2 * g + u) * HEAD_WIDTH
+                raw = lax.dot_general(
+                    keys, q_all[st, mi, :, first:first + HEAD_WIDTH],
+                    (((1,), (1,)), ((), ())), preferred_element_type=jnp.float32,
+                )
+                scores.append(jnp.where(masks[mi], raw, NEG))
+                c = (g * 2 + mi) * 2 + u
+                olds.append((m_ref[st, c:c + 1, :], l_ref[st, c:c + 1, :]))
+            results = []
+            for score, (old, share) in zip(scores, olds):
+                new = jnp.maximum(old, jnp.max(score, axis=0, keepdims=True))
+                weights = jnp.exp2((score - new) * SCALE2)
+                keep = jnp.exp2((old - new) * SCALE2)
+                share = share * keep + jnp.sum(weights, axis=0, keepdims=True)
+                mixed = jnp.dot(
+                    values, weights.astype(jnp.bfloat16), preferred_element_type=jnp.float32
+                )
+                results.append((new, share, keep, mixed))
+            for (mi, u), (new, share, keep, mixed) in zip(parts, results):
+                c = (g * 2 + mi) * 2 + u
+                m_ref[st, c:c + 1, :] = new
+                l_ref[st, c:c + 1, :] = share
+                acc[st, c] = acc[st, c] * keep + mixed
 
     member = x // 2
     mine = suffix_len[lax.rem(x, 2) * NZ + z]
@@ -248,6 +253,11 @@
             remote(
                 sending.at[i], kv.at[i], p_send.at[i], p_recv.at[i], partner
             ).wait_recv()
+
+        for k in range(2 + FLIGHT, PAGES):
+            @pl.when(i == k - FLIGHT)
+            def _():
+                p_copies[k].start()
 
         mask = rows < counts[i]
         attend(st, kv.at[i], {0: mask, 1: mask})
@@ -345,7 +355,7 @@
     swap.wait_recv()
     out_ref[...] = (own + sib_in[...].astype(jnp.float32)).astype(jnp.bfloat16)
 
-    for copy in q_copies + w_copies + p_copies + list(a_copies.values()) + [swap]:
+    for copy in q_copies + w_copies + p_copies[2:] + list(a_copies.values()) + [swap]:
         copy.wait_send()
     for pair in o_copies.values():
         for copy in pair:

time: 109 us -> 104 us (0.954)
  the two profiles are of different devices: /device:TPU:3 before, /device:TPU:5 now
where the time goes in v4:
time: 104 us
  Pallas kernels  102 us (98%)
  local copies, waits for them, and re-layouts  1.73 us (2%)
    pallas_call x1, Pallas kernels, shards(): pl.pallas_call(kernel, out_shape=jax.ShapeDtypeStruct((DEV_COLS, ROWS), b...  102 us

profile of v4, /device:TPU:5, one launch (start us, length us, event | category | flops | bytes accessed | tf_op | source)
XLA Modules:
  0.0 103.6 jit_solution(17225159646782820041)
XLA Ops:
  0.0 101.8 %paged_prefill.1 = bf16[672,256]{1,0:T(8,128)(2,1)} custom-call(s32[16,32]{1,0:T(8,128)} %owners.1, s32[16]{0:T(128)} %prefix_len.1, s32[16]{0:T(128)} %suffix_len.1, bf16[256,512]{1,0:T(8,128)(2,1)} %q_hbm.1, bf16[256,2,256]{2,1,0:T(2,128)(2,1)} %skv_hbm.1, bf16[16,256,2,256]{3,2,1,0:T(2,128)(2,1)} %pages_hbm.1, bf16[512,5376]{1,0:T(8,128)(2,1)} %w_hbm.1), custom_call_target="tpu_custom_call" | custom-call | tf_op jit(solution)/shard_map/paged_prefill/pallas_call | solution.py:369
  101.8 1.7 %copy.9 = bf16[256,672]{0,1:T(8,128)(2,1)} copy(bf16[256,672]{0,1:T(8,128)(2,1)} %bitcast.1) | data formatting | bytes 688128

commit v5 on v4

--- a/solution.py
+++ b/solution.py
@@ -22,14 +22,26 @@
 MESH = pl.DeviceIdType.MESH
 
 MESSAGES = (
-    ("h", 0, 0), ("s", 0, 0),
-    ("s", 0, 2), ("s", 2, 0), ("s", 2, 1), ("s", 3, 2), ("s", 1, 1),
-    ("s", 3, 1), ("s", 0, 1), ("s", 1, 0), ("s", 3, 0),
-    ("h", 1, 1), ("h", 1, -1), ("h", 1, 0), ("h", 0, 1), ("h", 0, -1),
+    ("h", 0, 0),
+    ("s", 0, 0),
+    ("s", 0, 2),
+    ("s", 1, 0),
+    ("s", 3, 0),
+    ("s", 0, 1),
+    ("s", 2, 0),
+    ("s", 1, 1),
+    ("s", 3, 1),
+    ("s", 3, 2),
+    ("s", 2, 1),
+    ("h", 0, 1),
+    ("h", 0, -1),
+    ("h", 1, 0),
+    ("h", 1, 1),
+    ("h", 1, -1),
 )
 SELF = (0, 1)
 SIDE_END = 11
-FLIGHT = 8
+FLIGHT = 10
 EARLY = 3
 
 
@@ -321,7 +333,7 @@
             first = (2 * g + u) * HEAD_WIDTH
             attn[y, :, first:first + HEAD_WIDTH] = value.T.astype(jnp.bfloat16)
         half = pl.ds(g * 256, 256)
-        for dy in (1, 3, 2):
+        for dy in (2, 1, 3):
             e = g * 3 + dy - 1
             copy = remote(
                 attn.at[y, :, half], attn.at[y, :, half], a_send.at[e], a_recv.at[e], chip(dy)

time: 104 us -> 101 us (0.971)
  the two profiles are of different devices: /device:TPU:5 before, /device:TPU:3 now
where the time goes in v5:
time: 101 us; the launch traced here: 99.6 us
  Pallas kernels  97.9 us (97%)
  local copies, waits for them, and re-layouts  1.73 us (2%)
    pallas_call x1, Pallas kernels, shards(): pl.pallas_call(kernel, out_shape=jax.ShapeDtypeStruct((DEV_COLS, ROWS), b...  97.9 us

profile of v5, /device:TPU:3, one launch (start us, length us, event | category | flops | bytes accessed | tf_op | source)
XLA Modules:
  0.0 99.6 jit_solution(8104747507224346778)
XLA Ops:
  0.0 97.9 %paged_prefill.1 = bf16[672,256]{1,0:T(8,128)(2,1)} custom-call(s32[16,32]{1,0:T(8,128)} %owners.1, s32[16]{0:T(128)} %prefix_len.1, s32[16]{0:T(128)} %suffix_len.1, bf16[256,512]{1,0:T(8,128)(2,1)} %q_hbm.1, bf16[256,2,256]{2,1,0:T(2,128)(2,1)} %skv_hbm.1, bf16[16,256,2,256]{3,2,1,0:T(2,128)(2,1)} %pages_hbm.1, bf16[512,5376]{1,0:T(8,128)(2,1)} %w_hbm.1), custom_call_target="tpu_custom_call" | custom-call | tf_op jit(solution)/shard_map/paged_prefill/pallas_call | solution.py:381
  97.9 1.7 %copy.9 = bf16[256,672]{0,1:T(8,128)(2,1)} copy(bf16[256,672]{0,1:T(8,128)(2,1)} %bitcast.1) | data formatting | bytes 688128

commit v6 on v5

--- a/solution.py
+++ b/solution.py
@@ -41,7 +41,7 @@
 )
 SELF = (0, 1)
 SIDE_END = 11
-FLIGHT = 10
+FLIGHT = 12
 EARLY = 3
 
 

time: 101 us -> 101 us (level)
  no operation moved by 1% of the time
where the time goes in v6:
time: 101 us; the launch traced here: 99.6 us
  Pallas kernels  97.9 us (97%)
  local copies, waits for them, and re-layouts  1.73 us (2%)
    pallas_call x1, Pallas kernels, shards(): pl.pallas_call(kernel, out_shape=jax.ShapeDtypeStruct((DEV_COLS, ROWS), b...  97.9 us

profile of v6, /device:TPU:3, one launch (start us, length us, event | category | flops | bytes accessed | tf_op | source)
XLA Modules:
  0.0 99.6 jit_solution(8241468237714672718)
XLA Ops:
  0.0 97.9 %paged_prefill.1 = bf16[672,256]{1,0:T(8,128)(2,1)} custom-call(s32[16,32]{1,0:T(8,128)} %owners.1, s32[16]{0:T(128)} %prefix_len.1, s32[16]{0:T(128)} %suffix_len.1, bf16[256,512]{1,0:T(8,128)(2,1)} %q_hbm.1, bf16[256,2,256]{2,1,0:T(2,128)(2,1)} %skv_hbm.1, bf16[16,256,2,256]{3,2,1,0:T(2,128)(2,1)} %pages_hbm.1, bf16[512,5376]{1,0:T(8,128)(2,1)} %w_hbm.1), custom_call_target="tpu_custom_call" | custom-call | tf_op jit(solution)/shard_map/paged_prefill/pallas_call | solution.py:381
  97.9 1.7 %copy.9 = bf16[256,672]{0,1:T(8,128)(2,1)} copy(bf16[256,672]{0,1:T(8,128)(2,1)} %bitcast.1) | data formatting | bytes 688128
